TPU v7x, 32 devices: a whole 2x2x4 slice. The times are simulated.
32 devices in a mesh: groups: 2 (over x), paths: 16 (over z, y, core).
Axes of the slice: x: 2, y: 2, z: 4, core: 2. Of those that a mesh axis runs over, the one named last changes fastest.
Arguments:
- path_basis: bfloat16 [4096, 512], P(('groups', 'paths')), parts along dimension 0, may hold values from -6 to 6
- proxy_weight: bfloat16 [4096, 512], P(('groups', 'paths')), parts along dimension 0, may hold values from -0.25 to 0.25
- notional: bfloat16 [4096], P(('groups', 'paths')), parts along dimension 0, may hold values from -4 to 4
- set_of: int32 [4096], P('groups'), parts along dimension 0, may hold values from 0 to 511
- threshold_index: int32 [1024], P('groups'), parts along dimension 0, may hold values from 0 to 15
- threshold_levels: float32 [32], P('groups'), parts along dimension 0, may hold values from 0.5 to 20
- loss_rate: float32 [1024], P('groups'), parts along dimension 0, may hold values from 0.4 to 1
Outputs:
- expected_loss: float32 [2], P('groups'), parts along dimension 0
- basis_adjoint: float32 [4096, 512], P(('groups', 'paths')), parts along dimension 0
- weight_adjoint: float32 [4096, 512], P(('groups', 'paths')), parts along dimension 0
There are 2 independent parts, one for each index of `groups`. A program takes and returns all parts, laid end to end along the dimension named above; each array names one. Nothing has to cross between parts.
Inputs may be any that keep to these rules, and one draw needn't show every extreme that they name: `set_of`: netting set of each trade; set sizes are uneven.
All inputs are finite; a program needn't handle non-finite values.
Results may differ from a plain program's by a relative error of at most 0.0041.
Values may be sent and summed in bfloat16 or wider, within the bound.
A program may use at most 64 MiB of HBM per device.

v0:
```python
import math

import jax
import jax.numpy as jnp
from jax import lax
from jax.sharding import PartitionSpec as P

REGRESSORS = 32


RIDGE_SCALE = 0.01
PRECISE = lax.Precision.HIGHEST


def table_rows(labels, classes, target_type):
    return (labels[:, None] == jnp.arange(classes, dtype=jnp.int32)[None, :]).astype(target_type)


def contract_rows(former, latter):
    return lax.dot_general(
        former,
        latter,
        (((0,), (0,)), ((), ())),
        precision=PRECISE,
        preferred_element_type=jnp.float32,
    )


def contract_cols(former, latter):
    return lax.dot_general(
        former,
        latter,
        (((1,), (1,)), ((), ())),
        precision=PRECISE,
        preferred_element_type=jnp.float32,
    )


def matrix_product(former, latter):
    return jnp.dot(former, latter, precision=PRECISE, preferred_element_type=jnp.float32)


def spd_solve(matrix, target):
    lower_factor = jnp.linalg.cholesky(matrix)
    halfway = lax.linalg.triangular_solve(lower_factor, target, left_side=True, lower=True)
    return lax.linalg.triangular_solve(
        lower_factor, halfway, left_side=True, lower=True, transpose_a=True
    )


def shards(
    path_basis, proxy_weight, notional, set_of, threshold_index, threshold_levels, loss_rate
):
    path_rows, feature_count = path_basis.shape
    paths_all = path_rows * lax.axis_size("paths")
    set_total = loss_rate.shape[0]
    design = jnp.concatenate(
        [
            jnp.ones((path_rows, 1), jnp.float32),
            path_basis[:, : REGRESSORS - 1].astype(jnp.float32),
        ],
        axis=1,
    )
    ridge_term = RIDGE_SCALE * paths_all * jnp.eye(REGRESSORS, dtype=jnp.float32)
    weight_all, notional_all = (
        lax.all_gather(proxy_weight, "paths", axis=0, tiled=True),
        lax.all_gather(notional, "paths", axis=0, tiled=True),
    )
    trade_count = weight_all.shape[0]
    block_cols = math.gcd(256, trade_count)
    block_count = trade_count // block_cols
    weight_blocks = weight_all.reshape(block_count, block_cols, feature_count)
    notional_blocks = notional_all.astype(jnp.float32).reshape(block_count, block_cols)
    set_blocks = set_of.reshape(block_count, block_cols)

    def forward_step(running, pieces):
        weight_block, notional_block, set_block = pieces
        pre_act = lax.dot_general(
            path_basis, weight_block, (((1,), (1,)), ((), ())), preferred_element_type=jnp.float32
        )
        trade_value = (notional_block[None, :] * jax.nn.softplus(pre_act)).astype(jnp.bfloat16)
        return (
            running
            + jnp.dot(
                trade_value,
                table_rows(set_block, set_total, jnp.bfloat16),
                preferred_element_type=jnp.float32,
            ),
            None,
        )

    exposure, _ = lax.scan(
        forward_step,
        jnp.zeros((path_rows, set_total), jnp.float32),
        (weight_blocks, notional_blocks, set_blocks),
    )
    thresholds = jnp.sum(
        table_rows(threshold_index, threshold_levels.shape[0], jnp.float32)
        * threshold_levels[None, :],
        axis=1,
    )
    set_columns = lax.all_to_all(exposure, "paths", split_axis=1, concat_axis=0, tiled=True)
    design_all = lax.all_gather(design, "paths", axis=0, tiled=True)
    local_sets = set_columns.shape[1]
    offset = lax.axis_index("paths") * local_sets
    thresh_here = lax.dynamic_slice_in_dim(thresholds, offset, local_sets)
    rate_here = lax.dynamic_slice_in_dim(loss_rate, offset, local_sets)
    gram_matrix = contract_rows(design_all, design_all) + ridge_term
    coeffs = spd_solve(gram_matrix, contract_rows(design_all, set_columns))
    fitted = matrix_product(design_all, coeffs)
    excess = fitted - thresh_here[None, :]
    seed_adjoint = rate_here[None, :] * jax.nn.sigmoid(excess)
    loss_sum = lax.psum(jnp.sum(rate_here[None, :] * jax.nn.softplus(excess)), "paths")
    solve_adjoint = spd_solve(gram_matrix, contract_rows(design_all, seed_adjoint))
    adjoint_full = matrix_product(design_all, solve_adjoint)
    exposure_adjoint = lax.all_to_all(
        adjoint_full.astype(jnp.bfloat16), "paths", split_axis=0, concat_axis=1, tiled=True
    )
    design_term = contract_cols(seed_adjoint - adjoint_full, coeffs) + contract_cols(
        set_columns - fitted, solve_adjoint
    )
    design_adjoint = lax.psum_scatter(design_term, "paths", scatter_dimension=0, tiled=True)
    expected_loss = (loss_sum / (paths_all * set_total)).reshape(1)

    def backward_step(running, pieces):
        weight_block, notional_block, set_block = pieces
        pre_trans = lax.dot_general(
            weight_block, path_basis, (((1,), (1,)), ((), ())), preferred_element_type=jnp.float32
        )
        spread_trans = lax.dot_general(
            table_rows(set_block, set_total, jnp.bfloat16),
            exposure_adjoint,
            (((1,), (1,)), ((), ())),
            preferred_element_type=jnp.float32,
        )
        slope_trans = (notional_block[:, None] * jax.nn.sigmoid(pre_trans) * spread_trans).astype(
            jnp.bfloat16
        )
        running = running + lax.dot_general(
            slope_trans, weight_block, (((0,), (0,)), ((), ())), preferred_element_type=jnp.float32
        )
        return (running, slope_trans)

    back_total, slope_stack = lax.scan(
        backward_step,
        jnp.zeros((path_rows, feature_count), jnp.float32),
        (weight_blocks, notional_blocks, set_blocks),
    )
    slopes = slope_stack.reshape(trade_count, path_rows)
    scale_factor = 1.0 / math.sqrt(paths_all)
    weight_adjoint = lax.psum_scatter(
        jnp.dot(slopes, path_basis, preferred_element_type=jnp.float32) * scale_factor,
        "paths",
        scatter_dimension=0,
        tiled=True,
    )
    padding = jnp.zeros((path_rows, feature_count - REGRESSORS + 1), jnp.float32)
    basis_adjoint = back_total + jnp.concatenate([design_adjoint[:, 1:], padding], axis=1)
    return (expected_loss, basis_adjoint, weight_adjoint)


def solution(mesh):
    placed = (
        P(("groups", "paths"), None),
        P(("groups", "paths"), None),
        P(("groups", "paths")),
        P("groups"),
        P("groups"),
        P("groups"),
        P("groups"),
    )
    return jax.shard_map(
        shards,
        mesh=mesh,
        in_specs=placed,
        out_specs=(P("groups"), P(("groups", "paths"), None), P(("groups", "paths"), None)),
        check_vma=False,
    )
```

profile of v0, /device:TPU:0, one launch (start us, length us, event | category | flops | bytes accessed | tf_op | source)
XLA Modules:
  0.0 245.0 jit_solution(9623423090362638424)
XLA Ops:
  7.2 0.7 all-gather.3.cloned.1.call-update
  7.9 0.7 reshape.60
  8.6 23.3 %all-gather = bf16[16,1,128]{2,1,0:T(2,128)(2,1)S(1)} all-gather(bf16[1,1,128]{2,1,0:T(2,128)(2,1)} %bitcast.126), channel_id=1, replica_groups=mesh['groups'=2,'paths'=16] {'paths'}, dimensions={0}, use_global_device_ids=true | all-gather | bytes 4352 | tf_op jit(solution)/shard_map/all_gather | solution.py:67
  31.9 0.8 slice.14
  32.8 23.1 %all_gather.9 = f32[2048,32]{1,0:T(8,128)S(1)} all-gather(f32[128,32]{1,0:T(8,128)S(1)} %pad_convert_fusion), channel_id=1, replica_groups=mesh['groups'=2,'paths'=16] {'paths'}, dimensions={0}, use_global_device_ids=true | all-gather | bytes 278528 | tf_op jit(solution)/shard_map/all_gather | solution.py:103
  55.9 1.8 convolution_add_fusion.3
  57.8 12.6 %while.24 = (s32[]{:T(128)}, f32[128,512]{1,0:T(8,128)S(1)}, f32[8,256]{1,0:T(8,128)S(1)}, bf16[8,256,512]{2,1,0:T(8,128)(2,1)}, bf16[128,512]{1,0:T(8,128)(2,1)...) while((s32[]{:T(128)}, f32[128,512]{1,0:T(8,128)S(1)}, f32[8,256]{1,0:T(8,128)S(1)}, ...), condition=%wide.region_3.5_spmd.clone, body=%wide.region_2.4_spmd.clone.sunk | while | flops 67633152 | bytes 923763 | solution.py:92
  57.9 1.5 convolution_add_fusion.6
  59.4 1.5 convolution_add_fusion.6
  61.0 1.5 convolution_add_fusion.6
  62.6 1.5 convolution_add_fusion.6
  64.2 1.5 convolution_add_fusion.6
  65.7 1.5 convolution_add_fusion.6
  67.3 1.5 convolution_add_fusion.6
  68.9 1.5 convolution_add_fusion.6
  70.4 0.8 copy.34
  71.3 5.4 %all-to-all-start = ((f32[128,16,32]{0,2,1:T(8,128)}), f32[128,16,32]{0,2,1:T(8,128)S(1)}, u32[]{:S(2)}, u32[]{:S(2)}) async-start(f32[128,16,32]{0,2,1:T(8,128)} %bitcast.7), calls=%async_computation | async-start | bytes 524288 | tf_op jit(solution)/shard_map/all_to_all | solution.py:102
  76.8 0.8 dynamic_slice.27
  77.6 2.9 %cholesky.18 = f32[32,32]{1,0:T(8,128)S(1)} custom-call(f32[32,32]{1,0:T(8,128)S(1)} %fusion.45), custom_call_target="Cholesky" | custom-call | tf_op jit(solution)/shard_map/jit(cholesky)/cholesky | solution.py:44
  80.5 0.6 compare_reduce_fusion
  81.2 0.7 fusion.36
  81.8 2.4 custom-call.13
  84.3 2.4 all-to-all-done
  86.7 1.8 fusion.30
  88.4 0.2 fusion.41
  88.8 1.9 fusion.29
  90.7 1.8 fusion.46
  92.5 0.2 fusion.37
  92.9 1.2 fusion.47
  94.1 0.7 copy_bitcast_fusion
  94.8 0.5 fusion.32
  95.3 3.7 %all-to-all-start.1 = ((bf16[16,128,32]{1,2,0:T(8,128)(2,1)}), bf16[16,128,32]{1,2,0:T(8,128)(2,1)S(1)}, u32[]{:S(2)}, u32[]{:S(2)}) async-start(bf16[16,128,32]{1,2,0:T(8,128)(2,1)} %copy_bitcast_fusion), calls=%async_computation.1 | async-start | bytes 262144 | tf_op jit(solution)/shard_map/all_to_all | solution.py:116
  99.1 1.1 convolution_add_fusion.2
  100.2 6.7 %all-to-all-done.1 = bf16[16,128,32]{1,2,0:T(8,128)(2,1)S(1)} async-done(((bf16[16,128,32]{1,2,0:T(8,128)(2,1)}), bf16[16,128,32]{1,2,0:T(8,128)(2,1)S(1)}, u32[]{:S(2)}, u32[]{:S(2)}) %all-to-all-start.1) | async-done | bytes 131104 | tf_op jit(solution)/shard_map/all_to_all | solution.py:116
  107.0 22.0 %while.25 = (s32[]{:T(128)}, f32[128,512]{1,0:T(8,128)S(1)}, bf16[8,256,128]{2,1,0:T(8,128)(2,1)S(1)}, f32[8,256]{1,0:T(8,128)S(1)}, bf16[8,256,512]{2,1,0:T(8,1...) while((s32[]{:T(128)}, f32[128,512]{1,0:T(8,128)S(1)}, ...), condition=%wide.region_8.12_spmd.clone, body=%wide.region_7.11_spmd.clone.sunk | while | flops 101122048 | bytes 1776771 | solution.py:144
  107.1 0.3 fusion.83
  107.4 1.2 bitcast_dynamic-update-slice_fusion.2
  108.6 1.2 convolution_add_fusion.7
  109.8 0.3 fusion.83
  110.1 1.2 bitcast_dynamic-update-slice_fusion.2
  111.3 1.2 convolution_add_fusion.7
  112.6 0.3 fusion.83
  112.9 1.2 bitcast_dynamic-update-slice_fusion.2
  114.1 1.2 convolution_add_fusion.7
  115.3 0.3 fusion.83
  115.6 1.2 bitcast_dynamic-update-slice_fusion.2
  116.8 1.2 convolution_add_fusion.7
  118.1 0.3 fusion.83
  118.4 1.2 bitcast_dynamic-update-slice_fusion.2
  119.6 1.2 convolution_add_fusion.7
  120.8 0.3 fusion.83
  121.1 1.2 bitcast_dynamic-update-slice_fusion.2
  122.3 1.2 convolution_add_fusion.7
  123.6 0.3 fusion.83
  123.9 1.2 bitcast_dynamic-update-slice_fusion.2
  125.1 1.2 convolution_add_fusion.7
  126.3 0.3 fusion.83
  126.6 1.2 bitcast_dynamic-update-slice_fusion.2
  127.8 1.2 convolution_add_fusion.7
  129.0 2.6 %convolution_multiply_fusion = f32[2048,512]{1,0:T(8,128)} fusion(bf16[2048,128]{1,0:T(8,128)(2,1)S(1)} %bitcast.120, bf16[128,512]{1,0:T(8,128)(2,1)S(1)} %get-tuple-element.356), kind=kOutput, calls=%fused_computation.35 | convolution fusion | flops 269484032 | bytes 4849664 | tf_op jit(solution)/shard_map/dot_general | solution.py:152
  131.7 31.0 %psum.7 = f32[]{:T(128)} all-reduce(f32[]{:T(128)} %get-tuple-element.198), channel_id=1, replica_groups=mesh['groups'=2,'paths'=16] {'paths'}, use_global_device_ids=true, to_apply=%region_6.10 | all-reduce | flops 1 | bytes 8 | tf_op jit(solution)/shard_map/psum | solution.py:113
  163.4 0.7 slice.16
  164.2 0.8 copy.39
  165.0 72.3 %reduce-scatter.5.cloned.1.call-done = f32[128,512]{1,0:T(8,128)} async-done(((f32[2048,512]{1,0:T(8,128)}), f32[128,512]{1,0:T(8,128)}) %reduce-scatter.5.cloned.1.call-update) | async-done | bytes 262160 | tf_op jit(solution)/shard_map/reduce_scatter | solution.py:151
  (61 shorter events, 1.4 us)
Async XLA Ops:
  7.2 50.6 %copy-start = (bf16[128,512]{1,0:T(8,128)(2,1)S(1)}, bf16[128,512]{1,0:T(8,128)(2,1)}, u32[]{:S(2)}) copy-start(bf16[128,512]{1,0:T(8,128)(2,1)} %param.16) | copy-start | bytes 393220
  7.2 50.6 %all-gather.3.cloned.1.call-start = ((), (), s32[]{:S(2)}) async-start(), calls=%async_computation.4 | async-start | bytes 2228224 | tf_op jit(solution)/shard_map/all_gather | solution.py:66
  57.8 18.9 %copy-start.1 = (s32[512]{0:T(512)S(1)}, s32[512]{0:T(512)}, u32[]{:S(2)}) copy-start(s32[512]{0:T(512)} %param.20) | copy-start | bytes 6148
  57.8 18.9 %copy-start.2 = (f32[16]{0:T(128)S(1)}, f32[16]{0:T(128)}, u32[]{:S(2)}) copy-start(f32[16]{0:T(128)} %param.21) | copy-start | bytes 196
  71.3 15.4 %all-to-all-start = ((f32[128,16,32]{0,2,1:T(8,128)}), f32[128,16,32]{0,2,1:T(8,128)S(1)}, u32[]{:S(2)}, u32[]{:S(2)}) async-start(f32[128,16,32]{0,2,1:T(8,128)} %bitcast.7), calls=%async_computation | async-start | bytes 524288 | tf_op jit(solution)/shard_map/all_to_all | solution.py:102
  95.3 11.6 %all-to-all-start.1 = ((bf16[16,128,32]{1,2,0:T(8,128)(2,1)}), bf16[16,128,32]{1,2,0:T(8,128)(2,1)S(1)}, u32[]{:S(2)}, u32[]{:S(2)}) async-start(bf16[16,128,32]{1,2,0:T(8,128)(2,1)} %copy_bitcast_fusion), calls=%async_computation.1 | async-start | bytes 262144 | tf_op jit(solution)/shard_map/all_to_all | solution.py:116
  99.0 64.4 %reduce-scatter.3.cloned.1.call-start = ((), (), s32[]{:S(2)}) async-start(), calls=%async_computation.5 | async-start | bytes 278528 | tf_op jit(solution)/shard_map/reduce_scatter | solution.py:122
  100.2 137.1 %reduce-scatter.5.cloned.1.call-start = ((), (), s32[]{:S(2)}) async-start(), calls=%async_computation.6 | async-start | bytes 4456448 | tf_op jit(solution)/shard_map/reduce_scatter | solution.py:151
Sparse Core Ops, SparseCore 0:
  10.1 45.6 all-gather.2
  103.9 57.0 reduce-scatter.2
  165.4 71.8 reduce-scatter.4
where the time goes:
time: 246 us; the launch traced here: 245 us
  waiting for transfers between devices  82.1 us (33%)
  blocking collectives  77.3 us (31%)
  matrix products  47.1 us (19%)
  between operations  15.7 us (6%)
  starting transfers between devices  9.16 us (4%)
  other arithmetic  7.58 us (3%)
  local copies, waits for them, and re-layouts  5.3 us (2%)
    reduce_scatter x1, waiting for transfers between devices, shards(): lax.psum_scatter(jnp.dot(slopes, path_basis, preferred_element_type=jnp.f...  72.3 us
    psum x1, blocking collectives, shards(): lax.psum(jnp.sum(rate_here[None, :] * jax.nn.softplus(excess)), 'paths')  31 us
    all_gather x1, blocking collectives, shards(): lax.all_gather(notional, 'paths', axis=0, tiled=True)  23.3 us
    all_gather x1, blocking collectives, shards(): design_all = lax.all_gather(design, 'paths', axis=0, tiled=True)  23.1 us
    dot_general x8, matrix products, forward_step(): jnp.dot(trade_value, table_rows(set_block, set_total, jnp.bfloat16), pref...  12.1 us
    dot_general x8, matrix products, backward_step(): lax.dot_general(weight_block, path_basis, (((1,), (1,)), ((), ())), prefe...  9.76 us
    dot_general x8, matrix products, backward_step(): lax.dot_general(slope_trans, weight_block, (((0,), (0,)), ((), ())), pref...  9.52 us
    all_to_all x1, waiting for transfers between devices, shards(): lax.all_to_all(adjoint_full.astype(jnp.bfloat16), 'paths', split_axis=0,...  6.71 us
  transfers between devices with their start and end apart: 5, of which 3 were waited for; matrix products, arithmetic and copies ran while one was open for 16% of the time, Pallas kernels for 0%

commit v1 on v0

v1 whole, which is shorter than its diff:
```python
import functools
import math

import jax
import jax.numpy as jnp
from jax import lax
from jax.experimental import pallas as pl
from jax.experimental.pallas import tpu as pltpu
from jax.sharding import PartitionSpec as P

REGRESSORS = 32
RIDGE_SCALE = 0.01
PRECISE = lax.Precision.HIGHEST
LANES = 128
F32 = jnp.float32
BF16 = jnp.bfloat16

NN = (((1,), (0,)), ((), ()))
NT = (((1,), (1,)), ((), ()))
TN = (((0,), (0,)), ((), ()))


def mm(a, b, dims=NN):
    return lax.dot_general(a, b, dims, preferred_element_type=F32)


def precise(a, b, dims=NN):
    return lax.dot_general(a, b, dims, precision=PRECISE, preferred_element_type=F32)


def split3(x):
    hi = x.astype(BF16)
    rest = x - hi.astype(F32)
    mid = rest.astype(BF16)
    lo = (rest - mid.astype(F32)).astype(BF16)
    return hi, mid, lo


def stack3(x):
    hi, mid, lo = split3(x)
    return jnp.concatenate([hi, mid, lo, jnp.zeros_like(hi)], axis=0)


def design_of(basis):
    front = pltpu.roll(basis[:, :LANES].astype(F32), 1, 1)
    lane = lax.broadcasted_iota(jnp.int32, front.shape, 1)
    return jnp.where(lane == 0, 1.0, jnp.where(lane < REGRESSORS, front, 0.0))


def triple(design):
    return (
        design + pltpu.roll(design, REGRESSORS, 1) + pltpu.roll(design, 2 * REGRESSORS, 1)
    ).astype(BF16)


def spd_inverse(gram):
    size = REGRESSORS
    row = lax.broadcasted_iota(jnp.int32, (size, LANES), 0)
    lane = lax.broadcasted_iota(jnp.int32, (size, LANES), 1)
    work = jnp.where(lane < size, gram, jnp.where(lane == row + size, 1.0, 0.0))
    for k in range(size):
        column = jnp.broadcast_to(work[:, k : k + 1], work.shape)
        pivot = work[k : k + 1, :] / column[k : k + 1, :]
        work = jnp.where(row == k, pivot, work - column * pivot)
    return pltpu.roll(work, LANES - size, 1)[:, :size]


def set_table(labels, set_total):
    sets = lax.broadcasted_iota(jnp.int32, (set_total, labels.shape[1]), 0)
    return jnp.where(sets == labels, 1.0, 0.0).astype(BF16)


def kernel(
    inner, outer, paths_all, set_total,
    pb_ref, w_ref, not_ref, set_ref, tidx_ref, level_ref, rate_ref,
    loss_ref, basis_ref, wadj_ref,
    pall, wall, nall, nsend, gown, gall, gqall, gqsend,
    bown, bq, bzsend, bz, ssend, sz, agsend, ag,
    eown, eq, wown, wz, pown, pq, nsig, tval,
    zsend, zrecv, qsend, qrecv,
):
    rows, feats = pb_ref.shape
    trades = w_ref.shape[0]
    quarter = set_total // inner
    me = lax.axis_index("paths")
    q = lax.rem(me, inner)
    z = lax.div(me, inner)

    def q_peer(d):
        return lax.rem(q + d, inner)

    def z_peer(d):
        return lax.rem(z + d, outer)

    barrier = pltpu.get_barrier_semaphore()
    for d in range(1, inner):
        pl.semaphore_signal(
            barrier, inc=1, device_id={"paths": z * inner + q_peer(d)},
            device_id_type=pl.DeviceIdType.MESH,
        )
    for d in range(1, outer):
        pl.semaphore_signal(
            barrier, inc=1, device_id={"paths": z_peer(d) * inner + q},
            device_id_type=pl.DeviceIdType.MESH,
        )

    pending = []

    def over_q(which, source, target):
        copies = []
        for d in range(1, inner):
            copy = pltpu.make_async_remote_copy(
                src_ref=source(q_peer(d)), dst_ref=target.at[q],
                send_sem=qsend.at[which, d - 1], recv_sem=qrecv.at[which, d - 1],
                device_id={"paths": z * inner + q_peer(d)},
                device_id_type=pl.DeviceIdType.MESH,
            )
            copy.start()
            copies.append(copy)
        pending.extend(copies)
        return copies

    def over_z(which, source, target):
        copies = []
        for d in range(1, outer):
            copy = pltpu.make_async_remote_copy(
                src_ref=source(z_peer(d)), dst_ref=target.at[z],
                send_sem=zsend.at[which, d - 1], recv_sem=zrecv.at[which, d - 1],
                device_id={"paths": z_peer(d) * inner + q},
                device_id_type=pl.DeviceIdType.MESH,
            )
            copy.start()
            copies.append(copy)
        pending.extend(copies)
        return copies

    def arrive(copies):
        for copy in copies:
            copy.wait_recv()

    def total(ref, count):
        result = ref[0].astype(F32)
        for i in range(1, count):
            result = result + ref[i].astype(F32)
        return result

    own_design = design_of(pb_ref[...])
    own_triple = triple(own_design)
    own_bf = own_design.astype(BF16)
    nrow = jnp.broadcast_to(not_ref[...].astype(F32), (8, trades))
    nsend[...] = nrow
    gram_own = mm(own_bf, own_bf, TN)[:REGRESSORS, :]
    gown[...] = gram_own
    pl.semaphore_wait(barrier, inner + outer - 2)

    gram_z = over_z(0, lambda peer: gown, gall)
    note_z = over_z(1, lambda peer: nsend, nall)
    path_q = over_q(0, lambda peer: pb_ref, pall)
    trade_z = over_z(2, lambda peer: w_ref, wall)
    gall[z] = gram_own
    nall[z] = nrow
    pall[q] = pb_ref[...]
    wall[z] = w_ref[...]

    arrive(gram_z)
    gram_mid = total(gall, outer)
    gqsend[...] = gram_mid
    gram_q = over_q(1, lambda peer: gqsend, gqall)
    gqall[q] = gram_mid

    thresholds = jnp.zeros((1, quarter), F32)
    levels = tidx_ref[pl.ds(q, 1), :]
    all_levels = tidx_ref[...]
    all_thresholds = jnp.zeros((inner, quarter), F32)
    for i in range(level_ref.shape[0]):
        thresholds = jnp.where(levels == i, level_ref[i], thresholds)
        all_thresholds = jnp.where(all_levels == i, level_ref[i], all_thresholds)
    rate = rate_ref[pl.ds(q, 1), :]
    all_rates = rate_ref[...]
    labels = jnp.concatenate(
        [set_ref[pl.ds(i * inner + q, 1), :] for i in range(outer)], axis=1
    )
    table = set_table(labels, set_total)

    arrive(path_q)
    paths = pall[...].reshape(inner * rows, feats)
    design = design_of(paths)
    design3 = triple(design)
    design_t = jnp.transpose(design)[:REGRESSORS, :].astype(BF16)

    arrive(gram_q)
    gram_row = lax.broadcasted_iota(jnp.int32, (REGRESSORS, LANES), 0)
    gram_lane = lax.broadcasted_iota(jnp.int32, (REGRESSORS, LANES), 1)
    ridge = jnp.where(gram_row == gram_lane, RIDGE_SCALE * paths_all, 0.0)
    inverse = spd_inverse(total(gqall, inner) + ridge)

    arrive(note_z)
    notional = jnp.concatenate([nall[i][0:1, :] for i in range(outer)], axis=1)
    arrive(trade_z)
    weights = wall[...].reshape(outer * trades, feats)
    pre_act = mm(paths, weights, NT)
    small = jnp.exp(-jnp.abs(pre_act))
    tval[...] = (notional * (jnp.maximum(pre_act, 0.0) + jnp.log1p(small))).astype(BF16)
    nsig[...] = notional * (jnp.where(pre_act >= 0.0, 1.0, small) / (1.0 + small))

    by_trade = mm(design_t, tval[...])
    by_set = mm(jnp.concatenate(split3(by_trade), axis=0), table, NT)
    moments = (
        by_set[:REGRESSORS] + by_set[REGRESSORS : 2 * REGRESSORS] + by_set[2 * REGRESSORS :]
    )
    for i in range(inner):
        bown[i] = moments[:, i * quarter : (i + 1) * quarter]
    moment_q = over_q(2, lambda peer: bown.at[peer], bq)
    bq[q] = bown[q]
    arrive(moment_q)
    moment_mid = total(bq, inner)
    bzsend[...] = moment_mid
    moment_z = over_z(3, lambda peer: bzsend, bz)
    bz[z] = moment_mid
    arrive(moment_z)
    coeffs = precise(inverse, total(bz, outer))
    excess = mm(design3, stack3(coeffs)) - thresholds
    fade = jnp.exp(-jnp.abs(excess))
    loss = jnp.maximum(excess, 0.0) + jnp.log1p(fade)
    seed = rate * (jnp.where(excess >= 0.0, 1.0, fade) / (1.0 + fade))
    loss_row = rate * jnp.sum(loss, axis=0, keepdims=True)
    seed_cut = mm(design_t, jnp.concatenate(split3(seed), axis=1))
    seed_sum = (
        seed_cut[:, :quarter] + seed_cut[:, quarter : 2 * quarter] + seed_cut[:, 2 * quarter :]
    )
    message = jnp.concatenate([seed_sum, jnp.broadcast_to(loss_row, (8, quarter))], axis=0)
    ssend[...] = message
    seed_z = over_z(4, lambda peer: ssend, sz)
    sz[z] = message
    arrive(seed_z)
    seed_total = total(sz, outer)
    solved = precise(inverse, seed_total[:REGRESSORS])
    answer = jnp.concatenate([coeffs, solved, seed_total[REGRESSORS:]], axis=0)
    agsend[...] = answer
    answer_q = over_q(3, lambda peer: agsend, ag)
    ag[q] = answer
    arrive(answer_q)
    answers = jnp.concatenate([ag[i] for i in range(inner)], axis=1)
    coeffs_all = answers[:REGRESSORS]
    solved_all = answers[REGRESSORS : 2 * REGRESSORS]
    loss_sum = jnp.sum(answers[2 * REGRESSORS : 2 * REGRESSORS + 1], axis=1, keepdims=True)
    loss_ref[...] = jnp.broadcast_to(loss_sum / (paths_all * set_total), loss_ref.shape)

    picked = mm(jnp.concatenate(split3(solved_all), axis=0), table)
    solved_at = (
        picked[:REGRESSORS] + picked[REGRESSORS : 2 * REGRESSORS] + picked[2 * REGRESSORS :]
    )
    solved3 = jnp.concatenate(
        [picked.astype(BF16), jnp.zeros((LANES - 3 * REGRESSORS, picked.shape[1]), BF16)], axis=0
    )
    spread = mm(design3, solved3).astype(BF16).astype(F32)
    slopes = (nsig[...] * spread).astype(BF16)
    scale = 1.0 / math.sqrt(paths_all)
    weight_part = mm(slopes, paths, TN) * scale
    wown[...] = weight_part.astype(BF16).reshape(outer, trades, feats)
    weight_z = over_z(5, lambda peer: wown.at[peer], wz)
    wz[z] = wown[z]

    pulled = mm(solved3, tval[...], NT)
    pulled = (
        pulled[:REGRESSORS]
        + pulled[REGRESSORS : 2 * REGRESSORS]
        + pulled[2 * REGRESSORS : 3 * REGRESSORS]
    )
    for i in range(inner):
        eown[i] = pulled[:, i * rows : (i + 1) * rows]
    pull_q = over_q(4, lambda peer: eown.at[peer], eq)
    eq[q] = eown[q]
    basis_part = mm(slopes, weights)
    pown[...] = basis_part.astype(BF16).reshape(inner, rows, feats)
    basis_q = over_q(5, lambda peer: pown.at[peer], pq)
    pq[q] = pown[q]

    fitted = mm(own_triple, stack3(coeffs_all))
    full_thresholds = jnp.concatenate([all_thresholds[i : i + 1] for i in range(inner)], axis=1)
    full_rates = jnp.concatenate([all_rates[i : i + 1] for i in range(inner)], axis=1)
    over = fitted - full_thresholds
    tail = jnp.exp(-jnp.abs(over))
    own_seed = full_rates * (jnp.where(over >= 0.0, 1.0, tail) / (1.0 + tail))
    residual = own_seed - mm(own_triple, stack3(solved_all))
    term = precise(coeffs_all, residual, NT) - precise(solved_all, fitted, NT)
    arrive(pull_q)
    term = term + total(eq, inner)
    padded = jnp.concatenate([term, jnp.zeros((LANES - REGRESSORS, rows), F32)], axis=0)
    turned = pltpu.roll(jnp.transpose(padded), LANES - 1, 1)
    lane = lax.broadcasted_iota(jnp.int32, turned.shape, 1)
    turned = jnp.where(lane < REGRESSORS - 1, turned, 0.0)
    arrive(basis_q)
    basis_ref[...] = total(pq, inner)
    basis_ref[:, :LANES] = basis_ref[:, :LANES] + turned
    arrive(weight_z)
    wadj_ref[...] = total(wz, outer)
    for copy in pending:
        copy.wait_send()


def shards(
    path_basis, proxy_weight, notional, set_of, threshold_index, threshold_levels, loss_rate
):
    count = lax.axis_size("paths")
    inner = math.gcd(4, count)
    outer = count // inner
    rows, feats = path_basis.shape
    trades = proxy_weight.shape[0]
    set_total = loss_rate.shape[0]
    quarter = set_total // inner
    size = REGRESSORS
    vmem = pl.BlockSpec(memory_space=pltpu.VMEM)
    z_pairs, q_pairs = max(outer - 1, 1), max(inner - 1, 1)
    loss, basis_adjoint, weight_adjoint = pl.pallas_call(
        functools.partial(kernel, inner, outer, rows * count, set_total),
        out_shape=(
            jax.ShapeDtypeStruct((1, LANES), F32),
            jax.ShapeDtypeStruct((rows, feats), F32),
            jax.ShapeDtypeStruct((trades, feats), F32),
        ),
        in_specs=[
            vmem, vmem, vmem, vmem, vmem, pl.BlockSpec(memory_space=pltpu.SMEM), vmem,
        ],
        out_specs=(vmem, vmem, vmem),
        scratch_shapes=[
            pltpu.VMEM((inner, rows, feats), BF16),
            pltpu.VMEM((outer, trades, feats), BF16),
            pltpu.VMEM((outer, 8, trades), F32),
            pltpu.VMEM((8, trades), F32),
            pltpu.VMEM((size, LANES), F32),
            pltpu.VMEM((outer, size, LANES), F32),
            pltpu.VMEM((inner, size, LANES), F32),
            pltpu.VMEM((size, LANES), F32),
            pltpu.VMEM((inner, size, quarter), F32),
            pltpu.VMEM((inner, size, quarter), F32),
            pltpu.VMEM((size, quarter), F32),
            pltpu.VMEM((outer, size, quarter), F32),
            pltpu.VMEM((size + 8, quarter), F32),
            pltpu.VMEM((outer, size + 8, quarter), F32),
            pltpu.VMEM((2 * size + 8, quarter), F32),
            pltpu.VMEM((inner, 2 * size + 8, quarter), F32),
            pltpu.VMEM((inner, size, rows), F32),
            pltpu.VMEM((inner, size, rows), F32),
            pltpu.VMEM((outer, trades, feats), BF16),
            pltpu.VMEM((outer, trades, feats), BF16),
            pltpu.VMEM((inner, rows, feats), BF16),
            pltpu.VMEM((inner, rows, feats), BF16),
            pltpu.VMEM((inner * rows, outer * trades), F32),
            pltpu.VMEM((inner * rows, outer * trades), BF16),
            pltpu.SemaphoreType.DMA((6, z_pairs)),
            pltpu.SemaphoreType.DMA((6, z_pairs)),
            pltpu.SemaphoreType.DMA((6, q_pairs)),
            pltpu.SemaphoreType.DMA((6, q_pairs)),
        ],
        compiler_params=pltpu.CompilerParams(
            collective_id=0, has_side_effects=True, vmem_limit_bytes=48 * 1024 * 1024
        ),
    )(
        path_basis,
        proxy_weight,
        notional.reshape(1, trades),
        set_of.reshape(-1, trades),
        threshold_index.reshape(inner, quarter),
        threshold_levels,
        loss_rate.reshape(inner, quarter),
    )
    return loss[0, :1], basis_adjoint, weight_adjoint


def solution(mesh):
    placed = (
        P(("groups", "paths"), None),
        P(("groups", "paths"), None),
        P(("groups", "paths")),
        P("groups"),
        P("groups"),
        P("groups"),
        P("groups"),
    )
    return jax.shard_map(
        shards,
        mesh=mesh,
        in_specs=placed,
        out_specs=(P("groups"), P(("groups", "paths"), None), P(("groups", "paths"), None)),
        check_vma=False,
    )
```

time: 246 us -> 54.9 us (0.22)
  waiting for transfers between devices: 82.1 us -> 0 us
  blocking collectives: 77.3 us -> 0 us
  Pallas kernels: 0 us -> 48.3 us
  matrix products: 47.1 us -> 0 us
  between operations: 15.7 us -> 1.84 us
  starting transfers between devices: 9.16 us -> 0 us
  other arithmetic: 7.58 us -> 0 us
    reduce_scatter x2 -> x0, waiting for transfers between devices: 72.3 us -> none  [the longest x1 72.3 us: shards(): lax.psum_scatter(jnp.dot(slopes, path_basis, preferred_element_type=jnp.f...]
    pallas_call x0 -> x1, Pallas kernels: none -> 48.3 us  [shards(): pl.pallas_call(functools.partial(kernel, inner, outer, rows * count, set_...]
    dot_general x40 -> x0, matrix products: 46.4 us -> none  [the longest x8 12.1 us: forward_step(): jnp.dot(trade_value, table_rows(set_block, set_total, jnp.bfloat16), pref...]
    all_gather x2 -> x0, blocking collectives: 46.3 us -> none  [the longest x1 23.3 us: shards(): lax.all_gather(notional, 'paths', axis=0, tiled=True)]
    psum x1 -> x0, blocking collectives: 31 us -> none  [shards(): lax.psum(jnp.sum(rate_here[None, :] * jax.nn.softplus(excess)), 'paths')]
    all_to_all x2 -> x0, waiting for transfers between devices: 9.1 us -> none  [the longest x1 6.71 us: shards(): lax.all_to_all(adjoint_full.astype(jnp.bfloat16), 'paths', split_axis=0,...]
    all_to_all x2 -> x0, starting transfers between devices: 9.04 us -> none  [the longest x1 5.38 us: shards(): lax.all_to_all(exposure, 'paths', split_axis=1, concat_axis=0, tiled=True)]
    another operation x5 -> x0, other arithmetic: 6.67 us -> none  [the longest x3 3.59 us: spd_solve(): lower_factor = jnp.linalg.cholesky(matrix)]
  transfers between devices with their start and end apart: 5 -> 0, of which waited for: 3 -> 0; matrix products, arithmetic and copies ran while one was open for 16% -> 0% of each run, Pallas kernels for 0% -> 0%
where the time goes in v1:
time: 54.9 us; the launch traced here: 54.7 us
  Pallas kernels  48.3 us (88%)
  local copies, waits for them, and re-layouts  4.58 us (8%)
  between operations  1.84 us (3%)
    pallas_call x1, Pallas kernels, shards(): pl.pallas_call(functools.partial(kernel, inner, outer, rows * count, set_...  48.3 us
    unnamed x16, local copies, waits for them, and re-layouts  4.58 us

profile of v1, /device:TPU:0, one launch (start us, length us, event | category | flops | bytes accessed | tf_op | source)
XLA Modules:
  0.0 54.7 jit_solution(17660729599390461546)
XLA Ops:
  0.6 0.0 copy-start.4
  0.6 0.0 copy-start.3
  0.7 0.0 copy-start.5
  0.7 0.0 copy-start.6
  0.7 0.6 %copy-done.4 = f32[512]{0:T(512)S(1)} copy-done((f32[512]{0:T(512)S(1)}, f32[512]{0:T(512)}, u32[]{:S(2)}) %copy-start.4) | copy-done | bytes 2072
  1.3 0.0 copy-done.3
  1.3 0.0 copy-done.5
  1.3 0.0 copy-done.6
  1.3 0.0 copy-start
  1.3 0.9 %copy-done = bf16[128,512]{1,0:T(8,128)(2,1)S(1)} copy-done((bf16[128,512]{1,0:T(8,128)(2,1)S(1)}, bf16[128,512]{1,0:T(8,128)(2,1)}, u32[]{:S(2)}) %copy-start) | copy-done | bytes 131096
  2.2 0.0 copy-start.1
  2.2 0.9 %copy-done.1 = bf16[128,512]{1,0:T(8,128)(2,1)S(1)} copy-done((bf16[128,512]{1,0:T(8,128)(2,1)S(1)}, bf16[128,512]{1,0:T(8,128)(2,1)}, u32[]{:S(2)}) %copy-start.1) | copy-done | bytes 131096
  3.1 0.0 copy-start.2
  3.1 0.7 %copy-done.2 = s32[2048]{0:T(1024)S(1)} copy-done((s32[2048]{0:T(1024)S(1)}, s32[2048]{0:T(1024)}, u32[]{:S(2)}) %copy-start.2) | copy-done | bytes 8216
  3.8 48.3 %shard_map.94 = (f32[1,128]{1,0:T(1,128)S(1)}, f32[128,512]{1,0:T(8,128)S(1)}, f32[128,512]{1,0:T(8,128)S(1)}) custom-call(bf16[128,512]{1,0:T(8,128)(2,1)S(1)} %copy-done, bf16[128,512]{1,0:T(8,128)(2,1)S(1)} %copy-done.1, bf16[1,128]{1,0:T(2,128)(2,1)S(1)} %bitcast.9, s32[16,128]{1,0:T(8,128)S(1)} %bitcast.6, s32[4,128]{1,0:T(4,128)S(1)} %bitcast.7, ...), custom_call_target="tpu_custom_call" | custom-call | tf_op jit(solution)/shard_map/pallas_call | solution.py:315
  52.2 0.7 %copy.14 = f32[128,512]{1,0:T(8,128)} copy(f32[128,512]{1,0:T(8,128)S(1)} %get-tuple-element.13) | data formatting | bytes 524288
  52.9 0.7 %copy.15 = f32[128,512]{1,0:T(8,128)} copy(f32[128,512]{1,0:T(8,128)S(1)} %get-tuple-element.14) | data formatting | bytes 524288
Async XLA Ops:
  0.6 0.7 %copy-start.4 = (f32[512]{0:T(512)S(1)}, f32[512]{0:T(512)}, u32[]{:S(2)}) copy-start(f32[512]{0:T(512)} %param.13) | copy-start | bytes 6148
  0.6 0.7 %copy-start.3 = (s32[512]{0:T(512)S(1)}, s32[512]{0:T(512)}, u32[]{:S(2)}) copy-start(s32[512]{0:T(512)} %param.11) | copy-start | bytes 6148
  0.7 0.7 %copy-start.5 = (bf16[128]{0:T(256)(128)(2,1)S(1)}, bf16[128]{0:T(256)(128)(2,1)}, u32[]{:S(2)}) copy-start(bf16[128]{0:T(256)(128)(2,1)} %param.9) | copy-start | bytes 772
  0.7 0.7 %copy-start.6 = (f32[16]{0:T(128)S(1)}, f32[16]{0:T(128)}, u32[]{:S(2)}) copy-start(f32[16]{0:T(128)} %level_ref.1) | copy-start | bytes 196
  1.3 0.9 %copy-start = (bf16[128,512]{1,0:T(8,128)(2,1)S(1)}, bf16[128,512]{1,0:T(8,128)(2,1)}, u32[]{:S(2)}) copy-start(bf16[128,512]{1,0:T(8,128)(2,1)} %pb_ref.1) | copy-start | bytes 393220
  2.2 0.9 %copy-start.1 = (bf16[128,512]{1,0:T(8,128)(2,1)S(1)}, bf16[128,512]{1,0:T(8,128)(2,1)}, u32[]{:S(2)}) copy-start(bf16[128,512]{1,0:T(8,128)(2,1)} %w_ref.1) | copy-start | bytes 393220
  3.1 0.7 %copy-start.2 = (s32[2048]{0:T(1024)S(1)}, s32[2048]{0:T(1024)}, u32[]{:S(2)}) copy-start(s32[2048]{0:T(1024)} %param.10) | copy-start | bytes 24580

commit v2 on v1

--- a/solution.py
+++ b/solution.py
@@ -62,7 +62,7 @@
         column = jnp.broadcast_to(work[:, k : k + 1], work.shape)
         pivot = work[k : k + 1, :] / column[k : k + 1, :]
         work = jnp.where(row == k, pivot, work - column * pivot)
-    return pltpu.roll(work, LANES - size, 1)[:, :size]
+    return pltpu.roll(work, LANES - size, 1)
 
 
 def set_table(labels, set_total):
@@ -70,37 +70,60 @@
     return jnp.where(sets == labels, 1.0, 0.0).astype(BF16)
 
 
+def partner(index, step, count):
+    if count & (count - 1):
+        return lax.rem(index + step, count)
+    result, weight = 0, 1
+    while weight < count:
+        bit = lax.rem(lax.div(index, weight), 2)
+        result = result + weight * (1 - bit if step & weight else bit)
+        weight *= 2
+    return result
+
+
 def kernel(
     inner, outer, paths_all, set_total,
-    pb_ref, w_ref, not_ref, set_ref, tidx_ref, level_ref, rate_ref,
+    pb_hbm, w_hbm, not_hbm, set_hbm, tidx_hbm, level_hbm, rate_hbm,
     loss_ref, basis_ref, wadj_ref,
-    pall, wall, nall, nsend, gown, gall, gqall, gqsend,
-    bown, bq, bzsend, bz, ssend, sz, agsend, ag,
+    not_ref, set_ref, tidx_ref, level_ref, rate_ref,
+    pall, wall, nall, nsend, gown, gall, gq, dstack, table, invert,
+    bown, bq, bzsend, bz, csend, cq, ssend, sq,
     eown, eq, wown, wz, pown, pq, nsig, tval,
-    zsend, zrecv, qsend, qrecv,
+    local, zsend, zrecv, qsend, qrecv,
 ):
-    rows, feats = pb_ref.shape
-    trades = w_ref.shape[0]
+    rows, feats = basis_ref.shape
+    trades = wadj_ref.shape[0]
     quarter = set_total // inner
     me = lax.axis_index("paths")
     q = lax.rem(me, inner)
     z = lax.div(me, inner)
 
-    def q_peer(d):
-        return lax.rem(q + d, inner)
-
-    def z_peer(d):
-        return lax.rem(z + d, outer)
+    loads = [
+        pltpu.make_async_copy(source, target, local.at[i])
+        for i, (source, target) in enumerate(
+            [
+                (pb_hbm, pall.at[q]),
+                (not_hbm, not_ref),
+                (w_hbm, wall.at[z]),
+                (set_hbm, set_ref),
+                (tidx_hbm, tidx_ref),
+                (level_hbm, level_ref),
+                (rate_hbm, rate_ref),
+            ]
+        )
+    ]
+    for load in loads:
+        load.start()
 
     barrier = pltpu.get_barrier_semaphore()
     for d in range(1, inner):
         pl.semaphore_signal(
-            barrier, inc=1, device_id={"paths": z * inner + q_peer(d)},
+            barrier, inc=1, device_id={"paths": z * inner + lax.rem(q + d, inner)},
             device_id_type=pl.DeviceIdType.MESH,
         )
     for d in range(1, outer):
         pl.semaphore_signal(
-            barrier, inc=1, device_id={"paths": z_peer(d) * inner + q},
+            barrier, inc=1, device_id={"paths": lax.rem(z + d, outer) * inner + q},
             device_id_type=pl.DeviceIdType.MESH,
         )
 
@@ -108,11 +131,12 @@
 
     def over_q(which, source, target):
         copies = []
-        for d in range(1, inner):
+        for d in range(inner - 1, 0, -1):
+            peer = partner(q, d, inner)
             copy = pltpu.make_async_remote_copy(
-                src_ref=source(q_peer(d)), dst_ref=target.at[q],
+                src_ref=source(peer), dst_ref=target.at[q],
                 send_sem=qsend.at[which, d - 1], recv_sem=qrecv.at[which, d - 1],
-                device_id={"paths": z * inner + q_peer(d)},
+                device_id={"paths": z * inner + peer},
                 device_id_type=pl.DeviceIdType.MESH,
             )
             copy.start()
@@ -122,11 +146,12 @@
 
     def over_z(which, source, target):
         copies = []
-        for d in range(1, outer):
+        for d in range(outer - 1, 0, -1):
+            peer = partner(z, d, outer)
             copy = pltpu.make_async_remote_copy(
-                src_ref=source(z_peer(d)), dst_ref=target.at[z],
+                src_ref=source(peer), dst_ref=target.at[z],
                 send_sem=zsend.at[which, d - 1], recv_sem=zrecv.at[which, d - 1],
-                device_id={"paths": z_peer(d) * inner + q},
+                device_id={"paths": peer * inner + q},
                 device_id_type=pl.DeviceIdType.MESH,
             )
             copy.start()
@@ -144,43 +169,46 @@
             result = result + ref[i].astype(F32)
         return result
 
-    own_design = design_of(pb_ref[...])
+    loads[0].wait()
+    own_design = design_of(pall[q])
     own_triple = triple(own_design)
-    own_bf = own_design.astype(BF16)
+    own_turned = jnp.transpose(own_design)[:REGRESSORS, :].astype(BF16)
+    gown[...] = own_turned
+    loads[1].wait()
     nrow = jnp.broadcast_to(not_ref[...].astype(F32), (8, trades))
     nsend[...] = nrow
-    gram_own = mm(own_bf, own_bf, TN)[:REGRESSORS, :]
-    gown[...] = gram_own
+    loads[2].wait()
     pl.semaphore_wait(barrier, inner + outer - 2)
 
     gram_z = over_z(0, lambda peer: gown, gall)
     note_z = over_z(1, lambda peer: nsend, nall)
-    path_q = over_q(0, lambda peer: pb_ref, pall)
-    trade_z = over_z(2, lambda peer: w_ref, wall)
-    gall[z] = gram_own
+    trade_z = over_z(2, lambda peer: wall.at[z], wall)
+    path_q = over_q(0, lambda peer: pall.at[q], pall)
+    gall[z] = own_turned
     nall[z] = nrow
-    pall[q] = pb_ref[...]
-    wall[z] = w_ref[...]
 
     arrive(gram_z)
-    gram_mid = total(gall, outer)
-    gqsend[...] = gram_mid
-    gram_q = over_q(1, lambda peer: gqsend, gqall)
-    gqall[q] = gram_mid
-
-    thresholds = jnp.zeros((1, quarter), F32)
-    levels = tidx_ref[pl.ds(q, 1), :]
+    gram_q = over_q(1, lambda peer: gall, gq)
+    gq[q] = gall[...]
+
+    for load in loads[3:]:
+        load.wait()
     all_levels = tidx_ref[...]
     all_thresholds = jnp.zeros((inner, quarter), F32)
+    levels = tidx_ref[pl.ds(q, 1), :]
+    thresholds = jnp.zeros((1, quarter), F32)
     for i in range(level_ref.shape[0]):
         thresholds = jnp.where(levels == i, level_ref[i], thresholds)
         all_thresholds = jnp.where(all_levels == i, level_ref[i], all_thresholds)
-    rate = rate_ref[pl.ds(q, 1), :]
+    thresholds = jnp.transpose(jnp.broadcast_to(thresholds, (quarter, quarter)))[:, :1]
+    rate = jnp.transpose(
+        jnp.broadcast_to(rate_ref[pl.ds(q, 1), :], (quarter, quarter))
+    )[:, :1]
     all_rates = rate_ref[...]
     labels = jnp.concatenate(
         [set_ref[pl.ds(i * inner + q, 1), :] for i in range(outer)], axis=1
     )
-    table = set_table(labels, set_total)
+    table[...] = set_table(labels, set_total)
 
     arrive(path_q)
     paths = pall[...].reshape(inner * rows, feats)
@@ -189,10 +217,17 @@
     design_t = jnp.transpose(design)[:REGRESSORS, :].astype(BF16)
 
     arrive(gram_q)
+    turned_all = jnp.concatenate(
+        [gq[i, j] for i in range(inner) for j in range(outer)], axis=1
+    )
+    dstack[...] = jnp.concatenate(
+        [turned_all, turned_all, turned_all, jnp.zeros_like(turned_all)], axis=0
+    )
+    gram = mm(turned_all, dstack[...], NT)
     gram_row = lax.broadcasted_iota(jnp.int32, (REGRESSORS, LANES), 0)
     gram_lane = lax.broadcasted_iota(jnp.int32, (REGRESSORS, LANES), 1)
     ridge = jnp.where(gram_row == gram_lane, RIDGE_SCALE * paths_all, 0.0)
-    inverse = spd_inverse(total(gqall, inner) + ridge)
+    invert[...] = spd_inverse(gram + ridge)
 
     arrive(note_z)
     notional = jnp.concatenate([nall[i][0:1, :] for i in range(outer)], axis=1)
@@ -204,7 +239,7 @@
     nsig[...] = notional * (jnp.where(pre_act >= 0.0, 1.0, small) / (1.0 + small))
 
     by_trade = mm(design_t, tval[...])
-    by_set = mm(jnp.concatenate(split3(by_trade), axis=0), table, NT)
+    by_set = mm(jnp.concatenate(split3(by_trade), axis=0), table[...], NT)
     moments = (
         by_set[:REGRESSORS] + by_set[REGRESSORS : 2 * REGRESSORS] + by_set[2 * REGRESSORS :]
     )
@@ -218,38 +253,34 @@
     moment_z = over_z(3, lambda peer: bzsend, bz)
     bz[z] = moment_mid
     arrive(moment_z)
+    inverse = invert[:, :REGRESSORS]
     coeffs = precise(inverse, total(bz, outer))
-    excess = mm(design3, stack3(coeffs)) - thresholds
+    csend[...] = coeffs
+    coeffs_q = over_q(3, lambda peer: csend, cq)
+    cq[q] = coeffs
+    excess = mm(stack3(coeffs), dstack[...], TN) - thresholds
     fade = jnp.exp(-jnp.abs(excess))
     loss = jnp.maximum(excess, 0.0) + jnp.log1p(fade)
     seed = rate * (jnp.where(excess >= 0.0, 1.0, fade) / (1.0 + fade))
-    loss_row = rate * jnp.sum(loss, axis=0, keepdims=True)
-    seed_cut = mm(design_t, jnp.concatenate(split3(seed), axis=1))
+    seed_cut = mm(dstack[:REGRESSORS, :], jnp.concatenate(split3(seed), axis=0), NT)
     seed_sum = (
         seed_cut[:, :quarter] + seed_cut[:, quarter : 2 * quarter] + seed_cut[:, 2 * quarter :]
     )
-    message = jnp.concatenate([seed_sum, jnp.broadcast_to(loss_row, (8, quarter))], axis=0)
-    ssend[...] = message
-    seed_z = over_z(4, lambda peer: ssend, sz)
-    sz[z] = message
-    arrive(seed_z)
-    seed_total = total(sz, outer)
-    solved = precise(inverse, seed_total[:REGRESSORS])
-    answer = jnp.concatenate([coeffs, solved, seed_total[REGRESSORS:]], axis=0)
-    agsend[...] = answer
-    answer_q = over_q(3, lambda peer: agsend, ag)
-    ag[q] = answer
+    solved = precise(inverse, seed_sum)
+    loss_part = jnp.sum(rate * jnp.sum(loss, axis=1, keepdims=True), axis=0, keepdims=True)
+    answer = jnp.concatenate([solved, jnp.broadcast_to(loss_part, (8, quarter))], axis=0)
+    ssend[...] = answer
+    answer_q = over_q(4, lambda peer: ssend, sq)
+    sq[q] = answer
+    arrive(coeffs_q)
+    coeffs_all = jnp.concatenate([cq[i] for i in range(inner)], axis=1)
     arrive(answer_q)
-    answers = jnp.concatenate([ag[i] for i in range(inner)], axis=1)
-    coeffs_all = answers[:REGRESSORS]
-    solved_all = answers[REGRESSORS : 2 * REGRESSORS]
-    loss_sum = jnp.sum(answers[2 * REGRESSORS : 2 * REGRESSORS + 1], axis=1, keepdims=True)
+    answers = jnp.concatenate([sq[i] for i in range(inner)], axis=1)
+    solved_all = answers[:REGRESSORS]
+    loss_sum = jnp.sum(answers[REGRESSORS : REGRESSORS + 1], axis=1, keepdims=True) / quarter
     loss_ref[...] = jnp.broadcast_to(loss_sum / (paths_all * set_total), loss_ref.shape)
 
-    picked = mm(jnp.concatenate(split3(solved_all), axis=0), table)
-    solved_at = (
-        picked[:REGRESSORS] + picked[REGRESSORS : 2 * REGRESSORS] + picked[2 * REGRESSORS :]
-    )
+    picked = mm(jnp.concatenate(split3(solved_all), axis=0), table[...])
     solved3 = jnp.concatenate(
         [picked.astype(BF16), jnp.zeros((LANES - 3 * REGRESSORS, picked.shape[1]), BF16)], axis=0
     )
@@ -258,7 +289,7 @@
     scale = 1.0 / math.sqrt(paths_all)
     weight_part = mm(slopes, paths, TN) * scale
     wown[...] = weight_part.astype(BF16).reshape(outer, trades, feats)
-    weight_z = over_z(5, lambda peer: wown.at[peer], wz)
+    weight_z = over_z(4, lambda peer: wown.at[peer], wz)
     wz[z] = wown[z]
 
     pulled = mm(solved3, tval[...], NT)
@@ -269,11 +300,11 @@
     )
     for i in range(inner):
         eown[i] = pulled[:, i * rows : (i + 1) * rows]
-    pull_q = over_q(4, lambda peer: eown.at[peer], eq)
+    pull_q = over_q(5, lambda peer: eown.at[peer], eq)
     eq[q] = eown[q]
     basis_part = mm(slopes, weights)
     pown[...] = basis_part.astype(BF16).reshape(inner, rows, feats)
-    basis_q = over_q(5, lambda peer: pown.at[peer], pq)
+    basis_q = over_q(6, lambda peer: pown.at[peer], pq)
     pq[q] = pown[q]
 
     fitted = mm(own_triple, stack3(coeffs_all))
@@ -319,27 +350,32 @@
             jax.ShapeDtypeStruct((rows, feats), F32),
             jax.ShapeDtypeStruct((trades, feats), F32),
         ),
-        in_specs=[
-            vmem, vmem, vmem, vmem, vmem, pl.BlockSpec(memory_space=pltpu.SMEM), vmem,
-        ],
+        in_specs=[pl.BlockSpec(memory_space=pltpu.HBM)] * 7,
         out_specs=(vmem, vmem, vmem),
         scratch_shapes=[
+            pltpu.VMEM((1, trades), BF16),
+            pltpu.VMEM((inner * outer, trades), jnp.int32),
+            pltpu.VMEM((inner, quarter), jnp.int32),
+            pltpu.SMEM(threshold_levels.shape, F32),
+            pltpu.VMEM((inner, quarter), F32),
             pltpu.VMEM((inner, rows, feats), BF16),
             pltpu.VMEM((outer, trades, feats), BF16),
             pltpu.VMEM((outer, 8, trades), F32),
             pltpu.VMEM((8, trades), F32),
-            pltpu.VMEM((size, LANES), F32),
-            pltpu.VMEM((outer, size, LANES), F32),
-            pltpu.VMEM((inner, size, LANES), F32),
+            pltpu.VMEM((size, rows), BF16),
+            pltpu.VMEM((outer, size, rows), BF16),
+            pltpu.VMEM((inner, outer, size, rows), BF16),
+            pltpu.VMEM((LANES, count * rows), BF16),
+            pltpu.VMEM((set_total, outer * trades), BF16),
             pltpu.VMEM((size, LANES), F32),
             pltpu.VMEM((inner, size, quarter), F32),
             pltpu.VMEM((inner, size, quarter), F32),
             pltpu.VMEM((size, quarter), F32),
             pltpu.VMEM((outer, size, quarter), F32),
+            pltpu.VMEM((size, quarter), F32),
+            pltpu.VMEM((inner, size, quarter), F32),
             pltpu.VMEM((size + 8, quarter), F32),
-            pltpu.VMEM((outer, size + 8, quarter), F32),
-            pltpu.VMEM((2 * size + 8, quarter), F32),
-            pltpu.VMEM((inner, 2 * size + 8, quarter), F32),
+            pltpu.VMEM((inner, size + 8, quarter), F32),
             pltpu.VMEM((inner, size, rows), F32),
             pltpu.VMEM((inner, size, rows), F32),
             pltpu.VMEM((outer, trades, feats), BF16),
@@ -348,13 +384,14 @@
             pltpu.VMEM((inner, rows, feats), BF16),
             pltpu.VMEM((inner * rows, outer * trades), F32),
             pltpu.VMEM((inner * rows, outer * trades), BF16),
-            pltpu.SemaphoreType.DMA((6, z_pairs)),
-            pltpu.SemaphoreType.DMA((6, z_pairs)),
-            pltpu.SemaphoreType.DMA((6, q_pairs)),
-            pltpu.SemaphoreType.DMA((6, q_pairs)),
+            pltpu.SemaphoreType.DMA((7,)),
+            pltpu.SemaphoreType.DMA((5, z_pairs)),
+            pltpu.SemaphoreType.DMA((5, z_pairs)),
+            pltpu.SemaphoreType.DMA((7, q_pairs)),
+            pltpu.SemaphoreType.DMA((7, q_pairs)),
         ],
         compiler_params=pltpu.CompilerParams(
-            collective_id=0, has_side_effects=True, vmem_limit_bytes=48 * 1024 * 1024
+            collective_id=0, has_side_effects=True, vmem_limit_bytes=67043328
         ),
     )(
         path_basis,

time: 54.9 us -> 52.8 us (0.962)
  local copies, waits for them, and re-layouts: 4.58 us -> 3.05 us
    unnamed x16 -> x6, local copies, waits for them, and re-layouts: 4.58 us -> 3.05 us
where the time goes in v2:
time: 52.8 us; the launch traced here: 52.7 us
  Pallas kernels  47.8 us (91%)
  local copies, waits for them, and re-layouts  3.05 us (6%)
  between operations  1.83 us (3%)
    pallas_call x1, Pallas kernels, shards(): pl.pallas_call(functools.partial(kernel, inner, outer, rows * count, set_...  47.8 us
    unnamed x6, local copies, waits for them, and re-layouts  3.05 us

profile of v2, /device:TPU:0, one launch (start us, length us, event | category | flops | bytes accessed | tf_op | source)
XLA Modules:
  0.0 52.7 jit_solution(18405030123171258911)
XLA Ops:
  0.6 47.8 %shard_map.94 = (f32[1,128]{1,0:T(1,128)}, f32[128,512]{1,0:T(8,128)}, f32[128,512]{1,0:T(8,128)}) custom-call(bf16[128,512]{1,0:T(8,128)(2,1)} %pb_hbm.1, bf16[128,512]{1,0:T(8,128)(2,1)} %w_hbm.1, bf16[1,128]{1,0:T(2,128)(2,1)} %bitcast.9, s32[16,128]{1,0:T(8,128)} %bitcast.6, s32[4,128]{1,0:T(4,128)} %bitcast.7, f32[16]{0:T(128)} %level_hbm.1, ...), custom_call_target="tpu_custom_call" | custom-call | tf_op jit(solution)/shard_map/pallas_call | solution.py:346
  48.4 0.0 copy-start.1
  48.4 0.6 %copy-done.1 = f32[1,128]{1,0:T(1,128)S(1)} copy-done((f32[1,128]{1,0:T(1,128)S(1)}, f32[1,128]{1,0:T(1,128)}, u32[]{:S(2)}) %copy-start.1) | copy-done | bytes 536
  49.1 0.0 copy-start
  49.1 1.7 %copy.14 = f32[128,512]{1,0:T(8,128)} copy(f32[128,512]{1,0:T(8,128)} %get-tuple-element.13) | data formatting | bytes 524288
  50.8 0.0 copy-done
  50.8 0.7 %copy.15 = f32[128,512]{1,0:T(8,128)} copy(f32[128,512]{1,0:T(8,128)S(1)} %copy-done) | data formatting | bytes 524288
Async XLA Ops:
  48.4 0.6 %copy-start.1 = (f32[1,128]{1,0:T(1,128)S(1)}, f32[1,128]{1,0:T(1,128)}, u32[]{:S(2)}) copy-start(f32[1,128]{1,0:T(1,128)} %get-tuple-element.6) | copy-start | bytes 1540
  49.1 1.7 %copy-start = (f32[128,512]{1,0:T(8,128)S(1)}, f32[128,512]{1,0:T(8,128)}, u32[]{:S(2)}) copy-start(f32[128,512]{1,0:T(8,128)} %get-tuple-element.14) | copy-start | bytes 786436

commit v3 on v2

--- a/solution.py
+++ b/solution.py
@@ -391,16 +391,21 @@
             pltpu.SemaphoreType.DMA((7, q_pairs)),
         ],
         compiler_params=pltpu.CompilerParams(
-            collective_id=0, has_side_effects=True, vmem_limit_bytes=67043328
+            collective_id=0, has_side_effects=True, vmem_limit_bytes=48 * 1024 * 1024
         ),
     )(
-        path_basis,
-        proxy_weight,
-        notional.reshape(1, trades),
-        set_of.reshape(-1, trades),
-        threshold_index.reshape(inner, quarter),
-        threshold_levels,
-        loss_rate.reshape(inner, quarter),
+        *(
+            pltpu.with_memory_space_constraint(operand, pltpu.HBM)
+            for operand in (
+                path_basis,
+                proxy_weight,
+                notional.reshape(1, trades),
+                set_of.reshape(-1, trades),
+                threshold_index.reshape(inner, quarter),
+                threshold_levels,
+                loss_rate.reshape(inner, quarter),
+            )
+        )
     )
     return loss[0, :1], basis_adjoint, weight_adjoint
 

time: 52.8 us -> 50.3 us (0.953)
  local copies, waits for them, and re-layouts: 3.05 us -> 1.41 us
  Pallas kernels: 47.8 us -> 47 us
    unnamed x6 -> x2, local copies, waits for them, and re-layouts: 3.05 us -> 1.41 us
    pallas_call x1, Pallas kernels: 47.8 us -> 47 us  [shards(): pl.pallas_call(functools.partial(kernel, inner, outer, rows * count, set_...]
where the time goes in v3:
time: 50.3 us; the launch traced here: 50.2 us
  Pallas kernels  47 us (93%)
  between operations  1.8 us (4%)
  local copies, waits for them, and re-layouts  1.41 us (3%)
    pallas_call x1, Pallas kernels, shards(): pl.pallas_call(functools.partial(kernel, inner, outer, rows * count, set_...  47 us
    unnamed x2, local copies, waits for them, and re-layouts  1.41 us

profile of v3, /device:TPU:0, one launch (start us, length us, event | category | flops | bytes accessed | tf_op | source)
XLA Modules:
  0.0 50.2 jit_solution(14001198482712261107)
XLA Ops:
  0.6 47.0 %shard_map.94 = (f32[1,128]{1,0:T(1,128)S(1)}, f32[128,512]{1,0:T(8,128)S(1)}, f32[128,512]{1,0:T(8,128)S(1)}) custom-call(bf16[128,512]{1,0:T(8,128)(2,1)} %pb_hbm.1, bf16[128,512]{1,0:T(8,128)(2,1)} %w_hbm.1, bf16[1,128]{1,0:T(2,128)(2,1)} %bitcast.10, s32[16,128]{1,0:T(8,128)} %bitcast.7, s32[4,128]{1,0:T(4,128)} %bitcast.8, f32[16]{0:T(128)} %level_hbm.1, ...), custom_call_target="tpu_custom_call" | custom-call | tf_op jit(solution)/shard_map/pallas_call | solution.py:346
  47.6 0.7 %copy.14 = f32[128,512]{1,0:T(8,128)} copy(f32[128,512]{1,0:T(8,128)S(1)} %get-tuple-element.13) | data formatting | bytes 524288
  48.3 0.7 %copy.15 = f32[128,512]{1,0:T(8,128)} copy(f32[128,512]{1,0:T(8,128)S(1)} %get-tuple-element.14) | data formatting | bytes 524288

commit v4 on v3

--- a/solution.py
+++ b/solution.py
@@ -12,6 +12,7 @@
 RIDGE_SCALE = 0.01
 PRECISE = lax.Precision.HIGHEST
 LANES = 128
+PIECES = 4
 F32 = jnp.float32
 BF16 = jnp.bfloat16
 
@@ -53,12 +54,14 @@
     ).astype(BF16)
 
 
-def spd_inverse(gram):
+def spd_inverse(gram, between):
     size = REGRESSORS
     row = lax.broadcasted_iota(jnp.int32, (size, LANES), 0)
     lane = lax.broadcasted_iota(jnp.int32, (size, LANES), 1)
     work = jnp.where(lane < size, gram, jnp.where(lane == row + size, 1.0, 0.0))
     for k in range(size):
+        if k == size // 3:
+            between()
         column = jnp.broadcast_to(work[:, k : k + 1], work.shape)
         pivot = work[k : k + 1, :] / column[k : k + 1, :]
         work = jnp.where(row == k, pivot, work - column * pivot)
@@ -89,7 +92,7 @@
     pall, wall, nall, nsend, gown, gall, gq, dstack, table, invert,
     bown, bq, bzsend, bz, csend, cq, ssend, sq,
     eown, eq, wown, wz, pown, pq, nsig, tval,
-    local, zsend, zrecv, qsend, qrecv,
+    via, local, zsend, zrecv, qsend, qrecv, steps,
 ):
     rows, feats = basis_ref.shape
     trades = wadj_ref.shape[0]
@@ -163,6 +166,26 @@
         for copy in copies:
             copy.wait_recv()
 
+    relay = outer == 4 and trades % (16 * PIECES) == 0
+    part = trades // PIECES
+    edge = z * (3 - z) == 0
+    near, far, mid = partner(z, 1, outer), partner(z, 2, outer), partner(z, 3, outer)
+
+    def piece(source, target, p, row, peer):
+        cut = pl.ds(p * part, part)
+        return pltpu.make_async_remote_copy(
+            src_ref=source.at[cut], dst_ref=target.at[cut],
+            send_sem=steps.at[row, p], recv_sem=steps.at[row + 1, p],
+            device_id={"paths": peer * inner + q}, device_id_type=pl.DeviceIdType.MESH,
+        )
+
+    def block(source, target, which, lane, peer):
+        return pltpu.make_async_remote_copy(
+            src_ref=source, dst_ref=target,
+            send_sem=zsend.at[which, lane], recv_sem=zrecv.at[which, lane],
+            device_id={"paths": peer * inner + q}, device_id_type=pl.DeviceIdType.MESH,
+        )
+
     def total(ref, count):
         result = ref[0].astype(F32)
         for i in range(1, count):
@@ -182,7 +205,30 @@
 
     gram_z = over_z(0, lambda peer: gown, gall)
     note_z = over_z(1, lambda peer: nsend, nall)
-    trade_z = over_z(2, lambda peer: wall.at[z], wall)
+    if relay:
+        far_in = [piece(wall.at[z], wall.at[z], p, 0, far) for p in range(PIECES)]
+        near_in = block(wall.at[z], wall.at[z], 2, 0, near)
+        mid_in = block(wall.at[z], wall.at[z], 2, 1, mid)
+        handed = [piece(wall.at[far], wall.at[far], p, 2, near) for p in range(PIECES)]
+        for copy in far_in:
+            copy.start()
+        near_in.start()
+        pending.extend(far_in + [near_in])
+
+        @pl.when(jnp.logical_not(edge))
+        def _():
+            mid_in.start()
+    else:
+        trade_z = over_z(2, lambda peer: wall.at[z], wall)
+
+    def forward(p):
+        if relay:
+            far_in[p].wait_recv()
+
+            @pl.when(jnp.logical_not(edge))
+            def _():
+                handed[p].start()
+
     path_q = over_q(0, lambda peer: pall.at[q], pall)
     gall[z] = own_turned
     nall[z] = nrow
@@ -210,12 +256,14 @@
     )
     table[...] = set_table(labels, set_total)
 
+    forward(0)
     arrive(path_q)
     paths = pall[...].reshape(inner * rows, feats)
     design = design_of(paths)
     design3 = triple(design)
     design_t = jnp.transpose(design)[:REGRESSORS, :].astype(BF16)
 
+    forward(1)
     arrive(gram_q)
     turned_all = jnp.concatenate(
         [gq[i, j] for i in range(inner) for j in range(outer)], axis=1
@@ -224,14 +272,27 @@
         [turned_all, turned_all, turned_all, jnp.zeros_like(turned_all)], axis=0
     )
     gram = mm(turned_all, dstack[...], NT)
+    forward(2)
     gram_row = lax.broadcasted_iota(jnp.int32, (REGRESSORS, LANES), 0)
     gram_lane = lax.broadcasted_iota(jnp.int32, (REGRESSORS, LANES), 1)
     ridge = jnp.where(gram_row == gram_lane, RIDGE_SCALE * paths_all, 0.0)
-    invert[...] = spd_inverse(gram + ridge)
+    invert[...] = spd_inverse(gram + ridge, lambda: forward(3))
 
     arrive(note_z)
     notional = jnp.concatenate([nall[i][0:1, :] for i in range(outer)], axis=1)
-    arrive(trade_z)
+    if relay:
+        near_in.wait_recv()
+
+        @pl.when(jnp.logical_not(edge))
+        def _():
+            mid_in.wait_recv()
+
+        @pl.when(edge)
+        def _():
+            for copy in handed:
+                copy.wait_recv()
+    else:
+        arrive(trade_z)
     weights = wall[...].reshape(outer * trades, feats)
     pre_act = mm(paths, weights, NT)
     small = jnp.exp(-jnp.abs(pre_act))
@@ -289,7 +350,28 @@
     scale = 1.0 / math.sqrt(paths_all)
     weight_part = mm(slopes, paths, TN) * scale
     wown[...] = weight_part.astype(BF16).reshape(outer, trades, feats)
-    weight_z = over_z(4, lambda peer: wown.at[peer], wz)
+    if relay:
+        carried = [piece(wown.at[mid], via, p, 6, near) for p in range(PIECES)]
+        far_out = [piece(wown.at[far], wz.at[z], p, 4, far) for p in range(PIECES)]
+        near_out = block(wown.at[near], wz.at[z], 4, 0, near)
+        mid_out = block(wown.at[mid], wz.at[z], 4, 1, mid)
+
+        @pl.when(edge)
+        def _():
+            for copy in carried:
+                copy.start()
+            for copy in far_out:
+                copy.start()
+            wz[mid] = jnp.zeros_like(via)
+
+        @pl.when(jnp.logical_not(edge))
+        def _():
+            mid_out.start()
+
+        near_out.start()
+        pending.extend(far_out + [near_out])
+    else:
+        weight_z = over_z(4, lambda peer: wown.at[peer], wz)
     wz[z] = wown[z]
 
     pulled = mm(solved3, tval[...], NT)
@@ -306,6 +388,17 @@
     pown[...] = basis_part.astype(BF16).reshape(inner, rows, feats)
     basis_q = over_q(6, lambda peer: pown.at[peer], pq)
     pq[q] = pown[q]
+
+    if relay:
+
+        @pl.when(jnp.logical_not(edge))
+        def _():
+            for p in range(PIECES):
+                carried[p].wait_recv()
+                cut = pl.ds(p * part, part)
+                joint = wown[far, cut, :].astype(F32) + via[cut, :].astype(F32)
+                wown[far, cut, :] = joint.astype(BF16)
+                far_out[p].start()
 
     fitted = mm(own_triple, stack3(coeffs_all))
     full_thresholds = jnp.concatenate([all_thresholds[i : i + 1] for i in range(inner)], axis=1)
@@ -324,7 +417,24 @@
     arrive(basis_q)
     basis_ref[...] = total(pq, inner)
     basis_ref[:, :LANES] = basis_ref[:, :LANES] + turned
-    arrive(weight_z)
+    if relay:
+        arrive(far_out)
+        near_out.wait_recv()
+
+        @pl.when(jnp.logical_not(edge))
+        def _():
+            mid_out.wait_recv()
+            mid_out.wait_send()
+            mid_in.wait_send()
+            for copy in handed:
+                copy.wait_send()
+
+        @pl.when(edge)
+        def _():
+            for copy in carried:
+                copy.wait_send()
+    else:
+        arrive(weight_z)
     wadj_ref[...] = total(wz, outer)
     for copy in pending:
         copy.wait_send()
@@ -384,11 +494,13 @@
             pltpu.VMEM((inner, rows, feats), BF16),
             pltpu.VMEM((inner * rows, outer * trades), F32),
             pltpu.VMEM((inner * rows, outer * trades), BF16),
+            pltpu.VMEM((trades, feats), BF16),
             pltpu.SemaphoreType.DMA((7,)),
             pltpu.SemaphoreType.DMA((5, z_pairs)),
             pltpu.SemaphoreType.DMA((5, z_pairs)),
             pltpu.SemaphoreType.DMA((7, q_pairs)),
             pltpu.SemaphoreType.DMA((7, q_pairs)),
+            pltpu.SemaphoreType.DMA((8, PIECES)),
         ],
         compiler_params=pltpu.CompilerParams(
             collective_id=0, has_side_effects=True, vmem_limit_bytes=48 * 1024 * 1024

time: 50.3 us -> 45.9 us (0.913)
  Pallas kernels: 47 us -> 42.6 us
    pallas_call x1, Pallas kernels: 47 us -> 42.6 us  [shards(): pl.pallas_call(functools.partial(kernel, inner, outer, rows * count, set_...]
where the time goes in v4:
time: 45.9 us; the launch traced here: 45.8 us
  Pallas kernels  42.6 us (93%)
  between operations  1.8 us (4%)
  local copies, waits for them, and re-layouts  1.41 us (3%)
    pallas_call x1, Pallas kernels, shards(): pl.pallas_call(functools.partial(kernel, inner, outer, rows * count, set_...  42.6 us
    unnamed x2, local copies, waits for them, and re-layouts  1.41 us

profile of v4, /device:TPU:0, one launch (start us, length us, event | category | flops | bytes accessed | tf_op | source)
XLA Modules:
  0.0 45.8 jit_solution(16725234106217560142)
XLA Ops:
  0.6 42.6 %shard_map.94 = (f32[1,128]{1,0:T(1,128)S(1)}, f32[128,512]{1,0:T(8,128)S(1)}, f32[128,512]{1,0:T(8,128)S(1)}) custom-call(bf16[128,512]{1,0:T(8,128)(2,1)} %pb_hbm.1, bf16[128,512]{1,0:T(8,128)(2,1)} %w_hbm.1, bf16[1,128]{1,0:T(2,128)(2,1)} %bitcast.10, s32[16,128]{1,0:T(8,128)} %bitcast.7, s32[4,128]{1,0:T(4,128)} %bitcast.8, f32[16]{0:T(128)} %level_hbm.1, ...), custom_call_target="tpu_custom_call" | custom-call | tf_op jit(solution)/shard_map/pallas_call | solution.py:456
  43.2 0.7 %copy.14 = f32[128,512]{1,0:T(8,128)} copy(f32[128,512]{1,0:T(8,128)S(1)} %get-tuple-element.13) | data formatting | bytes 524288
  44.0 0.7 %copy.15 = f32[128,512]{1,0:T(8,128)} copy(f32[128,512]{1,0:T(8,128)S(1)} %get-tuple-element.14) | data formatting | bytes 524288

commit v5 on v4

--- a/solution.py
+++ b/solution.py
@@ -90,7 +90,7 @@
     loss_ref, basis_ref, wadj_ref,
     not_ref, set_ref, tidx_ref, level_ref, rate_ref,
     pall, wall, nall, nsend, gown, gall, gq, dstack, table, invert,
-    bown, bq, bzsend, bz, csend, cq, ssend, sq,
+    bown, bq, bzsend, bz, csend, cq, ssend, sq, lsend, lq,
     eown, eq, wown, wz, pown, pq, nsig, tval,
     via, local, zsend, zrecv, qsend, qrecv, steps,
 ):
@@ -297,7 +297,6 @@
     pre_act = mm(paths, weights, NT)
     small = jnp.exp(-jnp.abs(pre_act))
     tval[...] = (notional * (jnp.maximum(pre_act, 0.0) + jnp.log1p(small))).astype(BF16)
-    nsig[...] = notional * (jnp.where(pre_act >= 0.0, 1.0, small) / (1.0 + small))
 
     by_trade = mm(design_t, tval[...])
     by_set = mm(jnp.concatenate(split3(by_trade), axis=0), table[...], NT)
@@ -308,6 +307,7 @@
         bown[i] = moments[:, i * quarter : (i + 1) * quarter]
     moment_q = over_q(2, lambda peer: bown.at[peer], bq)
     bq[q] = bown[q]
+    nsig[...] = notional * (jnp.where(pre_act >= 0.0, 1.0, small) / (1.0 + small))
     arrive(moment_q)
     moment_mid = total(bq, inner)
     bzsend[...] = moment_mid
@@ -321,25 +321,25 @@
     cq[q] = coeffs
     excess = mm(stack3(coeffs), dstack[...], TN) - thresholds
     fade = jnp.exp(-jnp.abs(excess))
-    loss = jnp.maximum(excess, 0.0) + jnp.log1p(fade)
     seed = rate * (jnp.where(excess >= 0.0, 1.0, fade) / (1.0 + fade))
     seed_cut = mm(dstack[:REGRESSORS, :], jnp.concatenate(split3(seed), axis=0), NT)
     seed_sum = (
         seed_cut[:, :quarter] + seed_cut[:, quarter : 2 * quarter] + seed_cut[:, 2 * quarter :]
     )
     solved = precise(inverse, seed_sum)
+    ssend[...] = solved
+    answer_q = over_q(4, lambda peer: ssend, sq)
+    sq[q] = solved
+    loss = jnp.maximum(excess, 0.0) + jnp.log1p(fade)
     loss_part = jnp.sum(rate * jnp.sum(loss, axis=1, keepdims=True), axis=0, keepdims=True)
-    answer = jnp.concatenate([solved, jnp.broadcast_to(loss_part, (8, quarter))], axis=0)
-    ssend[...] = answer
-    answer_q = over_q(4, lambda peer: ssend, sq)
-    sq[q] = answer
+    loss_row = jnp.broadcast_to(loss_part, (8, LANES))
+    lsend[...] = loss_row
+    loss_q = over_q(7, lambda peer: lsend, lq)
+    lq[q] = loss_row
     arrive(coeffs_q)
     coeffs_all = jnp.concatenate([cq[i] for i in range(inner)], axis=1)
     arrive(answer_q)
-    answers = jnp.concatenate([sq[i] for i in range(inner)], axis=1)
-    solved_all = answers[:REGRESSORS]
-    loss_sum = jnp.sum(answers[REGRESSORS : REGRESSORS + 1], axis=1, keepdims=True) / quarter
-    loss_ref[...] = jnp.broadcast_to(loss_sum / (paths_all * set_total), loss_ref.shape)
+    solved_all = jnp.concatenate([sq[i] for i in range(inner)], axis=1)
 
     picked = mm(jnp.concatenate(split3(solved_all), axis=0), table[...])
     solved3 = jnp.concatenate(
@@ -408,6 +408,8 @@
     own_seed = full_rates * (jnp.where(over >= 0.0, 1.0, tail) / (1.0 + tail))
     residual = own_seed - mm(own_triple, stack3(solved_all))
     term = precise(coeffs_all, residual, NT) - precise(solved_all, fitted, NT)
+    arrive(loss_q)
+    loss_ref[...] = total(lq, inner)[:1] / (paths_all * set_total)
     arrive(pull_q)
     term = term + total(eq, inner)
     padded = jnp.concatenate([term, jnp.zeros((LANES - REGRESSORS, rows), F32)], axis=0)
@@ -484,8 +486,10 @@
             pltpu.VMEM((outer, size, quarter), F32),
             pltpu.VMEM((size, quarter), F32),
             pltpu.VMEM((inner, size, quarter), F32),
-            pltpu.VMEM((size + 8, quarter), F32),
-            pltpu.VMEM((inner, size + 8, quarter), F32),
+            pltpu.VMEM((size, quarter), F32),
+            pltpu.VMEM((inner, size, quarter), F32),
+            pltpu.VMEM((8, LANES), F32),
+            pltpu.VMEM((inner, 8, LANES), F32),
             pltpu.VMEM((inner, size, rows), F32),
             pltpu.VMEM((inner, size, rows), F32),
             pltpu.VMEM((outer, trades, feats), BF16),
@@ -498,8 +502,8 @@
             pltpu.SemaphoreType.DMA((7,)),
             pltpu.SemaphoreType.DMA((5, z_pairs)),
             pltpu.SemaphoreType.DMA((5, z_pairs)),
-            pltpu.SemaphoreType.DMA((7, q_pairs)),
-            pltpu.SemaphoreType.DMA((7, q_pairs)),
+            pltpu.SemaphoreType.DMA((8, q_pairs)),
+            pltpu.SemaphoreType.DMA((8, q_pairs)),
             pltpu.SemaphoreType.DMA((8, PIECES)),
         ],
         compiler_params=pltpu.CompilerParams(

time: 45.9 us -> 45.9 us (level)
  no operation moved by 1% of the time
where the time goes in v5:
time: 45.9 us; the launch traced here: 45.8 us
  Pallas kernels  42.6 us (93%)
  between operations  1.8 us (4%)
  local copies, waits for them, and re-layouts  1.41 us (3%)
    pallas_call x1, Pallas kernels, shards(): pl.pallas_call(functools.partial(kernel, inner, outer, rows * count, set_...  42.6 us
    unnamed x2, local copies, waits for them, and re-layouts  1.41 us

profile of v5, /device:TPU:0, one launch (start us, length us, event | category | flops | bytes accessed | tf_op | source)
XLA Modules:
  0.0 45.8 jit_solution(15817399520128533835)
XLA Ops:
  0.6 42.6 %shard_map.94 = (f32[1,128]{1,0:T(1,128)S(1)}, f32[128,512]{1,0:T(8,128)S(1)}, f32[128,512]{1,0:T(8,128)S(1)}) custom-call(bf16[128,512]{1,0:T(8,128)(2,1)} %pb_hbm.1, bf16[128,512]{1,0:T(8,128)(2,1)} %w_hbm.1, bf16[1,128]{1,0:T(2,128)(2,1)} %bitcast.10, s32[16,128]{1,0:T(8,128)} %bitcast.7, s32[4,128]{1,0:T(4,128)} %bitcast.8, f32[16]{0:T(128)} %level_hbm.1, ...), custom_call_target="tpu_custom_call" | custom-call | tf_op jit(solution)/shard_map/pallas_call | solution.py:458
  43.3 0.7 %copy.14 = f32[128,512]{1,0:T(8,128)} copy(f32[128,512]{1,0:T(8,128)S(1)} %get-tuple-element.13) | data formatting | bytes 524288
  44.0 0.7 %copy.15 = f32[128,512]{1,0:T(8,128)} copy(f32[128,512]{1,0:T(8,128)S(1)} %get-tuple-element.14) | data formatting | bytes 524288

commit v6 on v5

--- a/solution.py
+++ b/solution.py
@@ -91,7 +91,7 @@
     not_ref, set_ref, tidx_ref, level_ref, rate_ref,
     pall, wall, nall, nsend, gown, gall, gq, dstack, table, invert,
     bown, bq, bzsend, bz, csend, cq, ssend, sq, lsend, lq,
-    eown, eq, wown, wz, pown, pq, nsig, tval,
+    eown, eq, wown, wz, pown, pq, nsig, tval, sval,
     via, local, zsend, zrecv, qsend, qrecv, steps,
 ):
     rows, feats = basis_ref.shape
@@ -166,7 +166,7 @@
         for copy in copies:
             copy.wait_recv()
 
-    relay = outer == 4 and trades % (16 * PIECES) == 0
+    relay = outer == 4 and trades % LANES == 0
     part = trades // PIECES
     edge = z * (3 - z) == 0
     near, far, mid = partner(z, 1, outer), partner(z, 2, outer), partner(z, 3, outer)
@@ -348,27 +348,43 @@
     spread = mm(design3, solved3).astype(BF16).astype(F32)
     slopes = (nsig[...] * spread).astype(BF16)
     scale = 1.0 / math.sqrt(paths_all)
-    weight_part = mm(slopes, paths, TN) * scale
-    wown[...] = weight_part.astype(BF16).reshape(outer, trades, feats)
+    sval[...] = slopes
+
+    def weigh(i):
+        columns = pl.ds(pl.multiple_of(i * trades, LANES), trades)
+        wown[i] = (mm(sval[:, columns], paths, TN) * scale).astype(BF16)
+
+    if not relay:
+        weight_part = mm(slopes, paths, TN) * scale
+        wown[...] = weight_part.astype(BF16).reshape(outer, trades, feats)
     if relay:
         carried = [piece(wown.at[mid], via, p, 6, near) for p in range(PIECES)]
         far_out = [piece(wown.at[far], wz.at[z], p, 4, far) for p in range(PIECES)]
         near_out = block(wown.at[near], wz.at[z], 4, 0, near)
         mid_out = block(wown.at[mid], wz.at[z], 4, 1, mid)
 
+        weigh(mid)
+
         @pl.when(edge)
         def _():
             for copy in carried:
                 copy.start()
+            wz[mid] = jnp.zeros_like(via)
+
+        @pl.when(jnp.logical_not(edge))
+        def _():
+            mid_out.start()
+
+        weigh(far)
+
+        @pl.when(edge)
+        def _():
             for copy in far_out:
                 copy.start()
-            wz[mid] = jnp.zeros_like(via)
-
-        @pl.when(jnp.logical_not(edge))
-        def _():
-            mid_out.start()
-
+
+        weigh(near)
         near_out.start()
+        weigh(z)
         pending.extend(far_out + [near_out])
     else:
         weight_z = over_z(4, lambda peer: wown.at[peer], wz)
@@ -498,6 +514,7 @@
             pltpu.VMEM((inner, rows, feats), BF16),
             pltpu.VMEM((inner * rows, outer * trades), F32),
             pltpu.VMEM((inner * rows, outer * trades), BF16),
+            pltpu.VMEM((inner * rows, outer * trades), BF16),
             pltpu.VMEM((trades, feats), BF16),
             pltpu.SemaphoreType.DMA((7,)),
             pltpu.SemaphoreType.DMA((5, z_pairs)),

time: 45.9 us -> 45.9 us (level)
  no operation moved by 1% of the time
where the time goes in v6:
time: 45.9 us; the launch traced here: 45.8 us
  Pallas kernels  42.5 us (93%)
  between operations  1.8 us (4%)
  local copies, waits for them, and re-layouts  1.41 us (3%)
    pallas_call x1, Pallas kernels, shards(): pl.pallas_call(functools.partial(kernel, inner, outer, rows * count, set_...  42.5 us
    unnamed x2, local copies, waits for them, and re-layouts  1.41 us

profile of v6, /device:TPU:0, one launch (start us, length us, event | category | flops | bytes accessed | tf_op | source)
XLA Modules:
  0.0 45.8 jit_solution(15788791185060232508)
XLA Ops:
  0.6 42.5 %shard_map.94 = (f32[1,128]{1,0:T(1,128)S(1)}, f32[128,512]{1,0:T(8,128)S(1)}, f32[128,512]{1,0:T(8,128)S(1)}) custom-call(bf16[128,512]{1,0:T(8,128)(2,1)} %pb_hbm.1, bf16[128,512]{1,0:T(8,128)(2,1)} %w_hbm.1, bf16[1,128]{1,0:T(2,128)(2,1)} %bitcast.10, s32[16,128]{1,0:T(8,128)} %bitcast.7, s32[4,128]{1,0:T(4,128)} %bitcast.8, f32[16]{0:T(128)} %level_hbm.1, ...), custom_call_target="tpu_custom_call" | custom-call | tf_op jit(solution)/shard_map/pallas_call | solution.py:474
  43.2 0.7 %copy.14 = f32[128,512]{1,0:T(8,128)} copy(f32[128,512]{1,0:T(8,128)S(1)} %get-tuple-element.13) | data formatting | bytes 524288
  43.9 0.7 %copy.15 = f32[128,512]{1,0:T(8,128)} copy(f32[128,512]{1,0:T(8,128)S(1)} %get-tuple-element.14) | data formatting | bytes 524288
